TPU v7x, 512 devices: a whole 4x4x16 slice. The times are simulated.
512 devices in a mesh: ctx: 64 (over y, z), ch: 8 (over x, core).
Axes of the slice: x: 4, y: 4, z: 16, core: 2. Of those that a mesh axis runs over, the one named last changes fastest.
Arguments:
- attn_proj: bfloat16 [8704, 3, 2048], P('ctx', None, 'ch'), may hold values from -40 to 40, as said below
- first_in: bfloat16 [8704, 3, 4096], P('ctx', None, 'ch'), may hold values from -6 to 6
- second_in: bfloat16 [8704, 3, 4096], P('ctx', None, 'ch'), may hold values from -6 to 6
- third_in: bfloat16 [8704, 3, 4096], P('ctx', None, 'ch'), may hold values from -6 to 6
- feat_filters: bfloat16 [3, 3, 3, 4096], P(None, None, None, 'ch'), may hold values from -3.5 to 3.5
- short_filters: bfloat16 [2, 7, 256], P(None, None, 'ch'), may hold values from -2 to 2
- long_filter: bfloat16 [128, 256], P('ch'), may hold values from -0.5 to 0.5
- positions: int32 [8704], P('ctx'), may hold values from 0 to 17406, as said below
Outputs:
- attn_out: bfloat16 [8704, 2048], P('ctx', 'ch')
- out_first: bfloat16 [8704, 4096], P('ctx', 'ch')
- out_second: bfloat16 [8704, 4096], P('ctx', 'ch')
- out_third: bfloat16 [8704, 4096], P('ctx', 'ch')
Inputs may be any that keep to these rules, and one draw needn't show every extreme that they name: `positions`: each token's position in its packed document: it rises by one from token to token and restarts at 0 at one to three tokens of the slice; the first token's value is how far its document began before the slice, at least 8704. `attn_proj`: entries of order one, except, in some draws, rows whose queries or keys are large.
All inputs are finite; a program needn't handle non-finite values.
Results may differ from a plain program's by a relative error of at most 0.0049.
Values may be sent and summed in bfloat16 or wider, within the bound.
A program may use at most 128 MiB of HBM per device.

v0:
```python
import math

import jax
import jax.numpy as jnp
from jax import lax
from jax.sharding import PartitionSpec as P

HD = 128
GROUP = 16


def from_behind(x, axis, by):
    peers = lax.axis_size(axis)
    pairs = [(i, i + by) for i in range(peers) if 0 <= i + by < peers]
    return lax.ppermute(x, axis, pairs)


def attend(attn_proj, positions):
    row_count = attn_proj.shape[0]
    channels = attn_proj.shape[2]
    head_count = channels // HD
    queries = attn_proj[:, 0].reshape(row_count, head_count, HD)
    key_value = attn_proj[:, 1:3]
    first_row = lax.axis_index("ctx") * row_count
    query_rows = first_row + jnp.arange(row_count, dtype=jnp.int32)
    doc_start = query_rows - positions
    score_scale = 1.0 / math.sqrt(HD)
    portion = lax.all_gather(key_value, "ctx", axis=0, tiled=True)
    count = portion.shape[0]
    old_peak = jnp.full((head_count, row_count), -1e30, jnp.float32)
    denominator = jnp.zeros((head_count, row_count), jnp.float32)
    numerator = jnp.zeros((head_count, row_count, HD), jnp.float32)
    key_rows = portion[:, 0].reshape(count, head_count, HD)
    value_rows = portion[:, 1].reshape(count, head_count, HD)
    source_rows = jnp.arange(count, dtype=jnp.int32)
    allowed = (source_rows[None, :] <= query_rows[:, None]) & (
        source_rows[None, :] >= doc_start[:, None]
    )
    scores = jnp.einsum("thd,shd->hts", queries, key_rows, preferred_element_type=jnp.float32)
    scores = jnp.where(allowed[None], scores * score_scale, -1e30)
    new_peak = jnp.maximum(jnp.maximum(old_peak, jnp.max(scores, axis=-1)), -1e20)
    weights = jnp.exp(scores - new_peak[:, :, None])
    rescale = jnp.exp(old_peak - new_peak)
    denominator = denominator * rescale + jnp.sum(weights, axis=-1)
    numerator = numerator * rescale[:, :, None] + jnp.einsum(
        "hts,shd->htd", weights.astype(jnp.bfloat16), value_rows, preferred_element_type=jnp.float32
    )
    final = (new_peak, denominator, numerator)
    denominator = final[1]
    numerator = final[2]
    result = numerator / denominator[:, :, None]
    return jnp.transpose(result, (1, 0, 2)).reshape(row_count, channels).astype(jnp.bfloat16)


def tap_sum(padded, filters, row_pos):
    tap_count = filters.shape[0]
    count = padded.shape[0] - (tap_count - 1)
    summed = jnp.zeros((count,) + padded.shape[1:], jnp.float32)
    for offset in range(tap_count):
        shifted = padded[tap_count - 1 - offset : tap_count - 1 - offset + count].astype(
            jnp.float32
        )
        in_doc = (
            (offset <= row_pos).astype(jnp.float32).reshape((count,) + (1,) * (padded.ndim - 1))
        )
        summed = summed + in_doc * filters[offset] * shifted
    return summed


def features(padded_raw, feat_filter, row_pos):
    featured = tap_sum(padded_raw, feat_filter.astype(jnp.float32), row_pos)
    return (featured[:, 0], (featured[:, 1] * featured[:, 2]).astype(jnp.bfloat16))


def banded_product(padded_mixed, filters, row_pos):
    span = filters.shape[0]
    count = row_pos.shape[0]
    total_rows = padded_mixed.shape[0]
    group_count = filters.shape[1]
    lag_table = (
        jnp.arange(count, dtype=jnp.int32)[:, None]
        + (total_rows - count)
        - jnp.arange(total_rows, dtype=jnp.int32)[None, :]
    )
    in_band = (lag_table >= 0) & (lag_table < span) & (lag_table <= row_pos[:, None])
    toeplitz = jnp.take(filters, jnp.clip(lag_table, 0, span - 1), axis=0)
    toeplitz = jnp.where(in_band[:, :, None], toeplitz, jnp.zeros((), filters.dtype))
    grouped = padded_mixed.reshape(total_rows, group_count, GROUP)
    result = jnp.einsum("tsg,sgc->tgc", toeplitz, grouped, preferred_element_type=jnp.float32)
    return result.reshape(count, group_count * GROUP)


def inner_conv(padded_mixed, inner_filter, row_pos, is_long):
    if is_long:
        return banded_product(padded_mixed, inner_filter, row_pos)
    expanded = jnp.repeat(inner_filter.astype(jnp.float32), GROUP, axis=1)
    return tap_sum(padded_mixed, expanded, row_pos)


def layer_apart(layer_in, feat_filter, inner_filter, positions, is_long):
    feat_count = feat_filter.shape[0]
    tap_count = inner_filter.shape[0]
    raw_rim = from_behind(layer_in[layer_in.shape[0] - (feat_count - 1) :], "ctx", 1)
    outer_gate, mixed_rows = features(
        jnp.concatenate([raw_rim, layer_in], axis=0), feat_filter, positions
    )
    tail_rows = mixed_rows[mixed_rows.shape[0] - (tap_count - 1) :]
    if is_long:
        mixed_rim = from_behind(tail_rows, "ctx", 1)
    else:
        mixed_rim = from_behind(tail_rows, "ctx", 1)
    padded_mixed = jnp.concatenate([mixed_rim, mixed_rows], axis=0)
    return (outer_gate * inner_conv(padded_mixed, inner_filter, positions, is_long)).astype(
        jnp.bfloat16
    )


def body(
    attn_proj, first_in, second_in, third_in, feat_filters, short_filters, long_filter, positions
):
    attn_out = attend(attn_proj, positions)
    long_taps = lax.all_to_all(long_filter, "ch", split_axis=1, concat_axis=0, tiled=True)
    out_first = layer_apart(first_in, feat_filters[0], short_filters[0], positions, False)
    out_second = layer_apart(second_in, feat_filters[1], short_filters[1], positions, False)
    out_third = layer_apart(third_in, feat_filters[2], long_taps, positions, True)
    return (attn_out, out_first, out_second, out_third)


def solution(mesh):
    in_specs = (
        P("ctx", None, "ch"),
        P("ctx", None, "ch"),
        P("ctx", None, "ch"),
        P("ctx", None, "ch"),
        P(None, None, None, "ch"),
        P(None, None, "ch"),
        P("ch", None),
        P("ctx"),
    )
    out_specs = (P("ctx", "ch"), P("ctx", "ch"), P("ctx", "ch"), P("ctx", "ch"))
    return jax.shard_map(body, mesh=mesh, in_specs=in_specs, out_specs=out_specs, check_vma=False)
```

profile of v0, /device:TPU:82, one launch (start us, length us, event | category | flops | bytes accessed | tf_op | source)
XLA Modules:
  0.0 280.7 jit_solution(5771420696352502964)
XLA Ops:
  7.2 1.0 slice.284
  8.2 0.8 copy.38
  9.0 0.8 slice.290
  9.7 3.8 %collective-permute-start = (bf16[2,3,512]{2,0,1:T(2,128)(2,1)S(1)}, bf16[2,3,512]{2,0,1:T(2,128)(2,1)S(1)}, u32[]{:S(2)}, u32[]{:S(2)}) collective-permute-start(bf16[2,3,512]{2,0,1:T(2,128)(2,1)S(1)} %slice.290), channel_id=1, source_target_pairs={{0,8},{8,16},{16,24},{24,32},{32,40},{40,48},{48,56},{56,64},{64,7... | collective-permute-start | bytes 18440 | tf_op jit(solution)/shard_map/ppermute | solution.py:15
  13.6 0.8 slice.356
  14.3 5.0 %collective-permute-start.4 = (bf16[2,3,512]{2,0,1:T(2,128)(2,1)S(1)}, bf16[2,3,512]{2,0,1:T(2,128)(2,1)S(1)}, u32[]{:S(2)}, u32[]{:S(2)}) collective-permute-start(bf16[2,3,512]{2,0,1:T(2,128)(2,1)S(1)} %slice.356), channel_id=1, source_target_pairs={{0,8},{8,16},{16,24},{24,32},{32,40},{40,48},{48,56},{56,64},{64,7... | collective-permute-start | bytes 18440 | tf_op jit(solution)/shard_map/ppermute | solution.py:15
  19.4 0.8 slice.323
  20.1 3.8 %collective-permute-start.2 = (bf16[2,3,512]{2,0,1:T(2,128)(2,1)S(1)}, bf16[2,3,512]{2,0,1:T(2,128)(2,1)S(1)}, u32[]{:S(2)}, u32[]{:S(2)}) collective-permute-start(bf16[2,3,512]{2,0,1:T(2,128)(2,1)S(1)} %slice.323), channel_id=1, source_target_pairs={{0,8},{8,16},{16,24},{24,32},{32,40},{40,48},{48,56},{56,64},{64,7... | collective-permute-start | bytes 18440 | tf_op jit(solution)/shard_map/ppermute | solution.py:15
  23.9 0.8 all_to_all.14
  24.8 0.7 reshape.340
  25.4 4.8 %all-to-all-start = ((bf16[8,2,256]{2,1,0:T(2,128)(2,1)}), bf16[8,2,256]{2,1,0:T(2,128)(2,1)}, u32[]{:S(2)}, u32[]{:S(2)}) async-start(bf16[8,2,256]{2,1,0:T(2,128)(2,1)} %reshape.340), calls=%async_computation | async-start | bytes 16384 | tf_op jit(solution)/shard_map/all_to_all | solution.py:122
  30.3 0.1 compare_select_fusion
  30.4 0.3 reshape.333
  30.8 0.7 iota_add_fusion.1
  31.4 1.3 compare_convert_fusion.3
  32.7 0.8 slice_convert_fusion.3
  33.5 0.7 slice_convert_fusion
  34.2 0.6 slice_bitcast_fusion.6
  34.8 1.5 fusion.48
  36.4 1.0 fusion.6
  37.4 0.9 slice.283
  38.3 0.7 reshape_squeeze.9
  41.2 1.9 multiply_add_fusion.2
  43.2 3.8 %collective-permute-start.1 = (bf16[6,512]{1,0:T(8,128)(2,1)S(1)}, bf16[6,512]{1,0:T(8,128)(2,1)S(1)}, u32[]{:S(2)}, u32[]{:S(2)}) collective-permute-start(bf16[6,512]{1,0:T(8,128)(2,1)S(1)} %slice_bitcast_fusion.11), channel_id=1, source_target_pairs={{0,8},{8,16},{16,24},{24,32},{32,40},{40,48},{48,56},{56,64},{64,7... | collective-permute-start | bytes 18440 | tf_op jit(solution)/shard_map/ppermute | solution.py:15
  47.1 0.6 copy-done.13
  47.6 2.4 multiply_add_fusion
  50.1 0.7 slice_bitcast_fusion.7
  50.8 3.8 %collective-permute-start.3 = (bf16[6,512]{1,0:T(8,128)(2,1)}, bf16[6,512]{1,0:T(8,128)(2,1)S(1)}, u32[]{:S(2)}, u32[]{:S(2)}) collective-permute-start(bf16[6,512]{1,0:T(8,128)(2,1)} %slice_bitcast_fusion.7), channel_id=1, source_target_pairs={{0,8},{8,16},{16,24},{24,32},{32,40},{40,48},{48,56},{56,64},{64,7... | collective-permute-start | bytes 18440 | tf_op jit(solution)/shard_map/ppermute | solution.py:15
  54.8 0.7 slice_bitcast_fusion.3
  55.5 5.2 %collective-permute-start.5 = (bf16[127,512]{1,0:T(8,128)(2,1)}, bf16[127,512]{1,0:T(8,128)(2,1)}, u32[]{:S(2)}, u32[]{:S(2)}) collective-permute-start(bf16[127,512]{1,0:T(8,128)(2,1)} %slice_bitcast_fusion.3), channel_id=1, source_target_pairs={{0,8},{8,16},{16,24},{24,32},{32,40},{40,48},{48,56},{56,64},{64,7... | collective-permute-start | bytes 390152 | tf_op jit(solution)/shard_map/ppermute | solution.py:15
  60.7 0.8 reshape.341
  61.5 124.8 %gather_fusion = bf16[35768,32]{1,0:T(8,128)(2,1)} fusion(bf16[128,32]{1,0:T(8,128)(2,1)S(1)} %bitcast.119, s32[35840]{0:T(1024)S(1)} %pad_clamp_fusion), kind=kCustom, calls=%fused_computation | custom fusion | bytes 4721376 | tf_op jit(solution)/shard_map/jit(_take)/gather | solution.py:86
  186.3 8.4 %copy.34 = bf16[35768,32]{0,1:T(8,128)(2,1)} copy(bf16[35768,32]{1,0:T(8,128)(2,1)} %gather_fusion) | data formatting | bytes 4578304 | tf_op jit(solution)/shard_map/jit(_take)/gather | solution.py:86
  194.7 6.6 %reshape.332 = bf16[136,263,32]{1,0,2:T(8,128)(2,1)} reshape(bf16[35768,32]{0,1:T(8,128)(2,1)} %copy.34) | data formatting | bytes 4578304 | tf_op jit(solution)/shard_map/jit(_take)/gather | solution.py:86
  201.3 1.0 fusion.40
  202.4 2.0 fusion.37
  204.3 0.9 pad_maximum_fusion.3
  205.3 0.2 copy.32
  205.5 3.3 %fusion.7 = f32[32,16,136]{2,1,0:T(8,128)S(1)} fusion(bf16[263,32,16]{0,2,1:T(8,128)(2,1)S(1)} %bitcast.125, bf16[136,263,32]{1,0,2:T(8,128)(2,1)} %reshape.332, pred[136,263]{1,0:T(8,128)(4,1)S(1)} %copy-done.4, pred[136,263]{1,0:T(8,128)(4,1)S(1)} %copy-done.3), kind=kOutput, calls=%fused_computation.11 | convolution fusion | flops 38915584 | bytes 2908528 | tf_op jit(solution)/shard_map/tsg,sgc->tgc/dot_general | solution.py:89
  208.8 0.2 copy.35
  209.0 0.7 fusion.34
  209.7 18.7 %fusion.63 = (bf16[8704,1,256]{2,1,0:T(2,128)(2,1)}, bf16[8704,1,256]{2,1,0:T(2,128)(2,1)}) fusion(bf16[8704,2,256]{2,1,0:T(2,128)(2,1)} %all-gather.2.cloned.1.call-done), kind=kLoop, calls=%fused_computation.142 | loop fusion | bytes 17825792 | tf_op jit(solution)/shard_map/slice | solution.py:33
  228.4 18.6 %copy.40 = bf16[8704,1,256]{0,2,1:T(8,128)(2,1)} copy(bf16[8704,1,256]{2,1,0:T(2,128)(2,1)} %get-tuple-element.5) | data formatting | bytes 8912896
  247.0 18.5 %copy.39 = bf16[8704,1,256]{0,2,1:T(8,128)(2,1)} copy(bf16[8704,1,256]{2,1,0:T(2,128)(2,1)} %get-tuple-element.4) | data formatting | bytes 8912896
  265.5 4.4 %fusion.64 = (f32[2,136]{1,0:T(2,128)S(1)}, f32[2,136,8704]{2,1,0:T(8,128)S(1)}) fusion(bf16[8704,2,128]{0,2,1:T(8,128)(2,1)} %bitcast.120, bf16[136,2,128]{2,1,0:T(2,128)(2,1)S(1)} %copy-done.2, pred[136,8704]{1,0:T(8,128)(4,1)S(1)} %fusion.6), kind=kOutput, calls=%fused_computation.143 | convolution fusion | flops 613179136 | bytes 15180864 | tf_op jit(solution)/shard_map/thd,shd->hts/dot_general | solution.py:39
  269.9 1.5 fusion.1
  271.4 1.7 fusion.26
  273.2 0.6 copy.48
  (86 shorter events, 2.6 us)
Async XLA Ops:
  7.2 40.5 %copy-start.1 = (bf16[136,3,512]{2,0,1:T(8,128)(2,1)S(1)}, bf16[136,3,512]{2,0,1:T(8,128)(2,1)}, u32[]{:S(2)}) copy-start(bf16[136,3,512]{2,0,1:T(8,128)(2,1)} %param.11) | copy-start | bytes 1253380
  7.2 202.5 %all-gather.2.cloned.1.call-start = ((), (), s32[]{:S(2)}) async-start(), calls=%async_computation.1 | async-start | bytes 9052160 | tf_op jit(solution)/shard_map/all_gather | solution.py:28
  9.7 31.4 %collective-permute-start = (bf16[2,3,512]{2,0,1:T(2,128)(2,1)S(1)}, bf16[2,3,512]{2,0,1:T(2,128)(2,1)S(1)}, u32[]{:S(2)}, u32[]{:S(2)}) collective-permute-start(bf16[2,3,512]{2,0,1:T(2,128)(2,1)S(1)} %slice.290), channel_id=1, source_target_pairs={{0,8},{8,16},{16,24},{24,32},{32,40},{40,48},{48,56},{56,64},{64,7... | collective-permute-start | bytes 18440 | tf_op jit(solution)/shard_map/ppermute | solution.py:15
  14.3 32.7 %collective-permute-start.4 = (bf16[2,3,512]{2,0,1:T(2,128)(2,1)S(1)}, bf16[2,3,512]{2,0,1:T(2,128)(2,1)S(1)}, u32[]{:S(2)}, u32[]{:S(2)}) collective-permute-start(bf16[2,3,512]{2,0,1:T(2,128)(2,1)S(1)} %slice.356), channel_id=1, source_target_pairs={{0,8},{8,16},{16,24},{24,32},{32,40},{40,48},{48,56},{56,64},{64,7... | collective-permute-start | bytes 18440 | tf_op jit(solution)/shard_map/ppermute | solution.py:15
  20.1 26.9 %collective-permute-start.2 = (bf16[2,3,512]{2,0,1:T(2,128)(2,1)S(1)}, bf16[2,3,512]{2,0,1:T(2,128)(2,1)S(1)}, u32[]{:S(2)}, u32[]{:S(2)}) collective-permute-start(bf16[2,3,512]{2,0,1:T(2,128)(2,1)S(1)} %slice.323), channel_id=1, source_target_pairs={{0,8},{8,16},{16,24},{24,32},{32,40},{40,48},{48,56},{56,64},{64,7... | collective-permute-start | bytes 18440 | tf_op jit(solution)/shard_map/ppermute | solution.py:15
  25.4 35.2 %all-to-all-start = ((bf16[8,2,256]{2,1,0:T(2,128)(2,1)}), bf16[8,2,256]{2,1,0:T(2,128)(2,1)}, u32[]{:S(2)}, u32[]{:S(2)}) async-start(bf16[8,2,256]{2,1,0:T(2,128)(2,1)} %reshape.340), calls=%async_computation | async-start | bytes 16384 | tf_op jit(solution)/shard_map/all_to_all | solution.py:122
  32.7 8.5 %copy-start.5 = (f32[136]{0:T(256)}, f32[136]{0:T(256)S(1)}, u32[]{:S(2)}) copy-start(f32[136]{0:T(256)S(1)} %get-tuple-element.44) | copy-start | bytes 1636
  32.7 8.5 %copy-start.7 = (f32[136]{0:T(256)}, f32[136]{0:T(256)S(1)}, u32[]{:S(2)}) copy-start(f32[136]{0:T(256)S(1)} %get-tuple-element.45) | copy-start | bytes 1636
  43.2 158.1 %collective-permute-start.1 = (bf16[6,512]{1,0:T(8,128)(2,1)S(1)}, bf16[6,512]{1,0:T(8,128)(2,1)S(1)}, u32[]{:S(2)}, u32[]{:S(2)}) collective-permute-start(bf16[6,512]{1,0:T(8,128)(2,1)S(1)} %slice_bitcast_fusion.11), channel_id=1, source_target_pairs={{0,8},{8,16},{16,24},{24,32},{32,40},{40,48},{48,56},{56,64},{64,7... | collective-permute-start | bytes 18440 | tf_op jit(solution)/shard_map/ppermute | solution.py:15
  47.0 0.6 copy-start.13
  47.0 0.6 copy-start.14
  50.0 4.6 %copy-start = (f32[136,3,512]{2,0,1:T(8,128)}, f32[136,3,512]{2,0,1:T(8,128)S(1)}, u32[]{:S(2)}) copy-start(f32[136,3,512]{2,0,1:T(8,128)S(1)} %get-tuple-element.35) | copy-start | bytes 2506756
  50.8 151.6 %collective-permute-start.3 = (bf16[6,512]{1,0:T(8,128)(2,1)}, bf16[6,512]{1,0:T(8,128)(2,1)S(1)}, u32[]{:S(2)}, u32[]{:S(2)}) collective-permute-start(bf16[6,512]{1,0:T(8,128)(2,1)} %slice_bitcast_fusion.7), channel_id=1, source_target_pairs={{0,8},{8,16},{16,24},{24,32},{32,40},{40,48},{48,56},{56,64},{64,7... | collective-permute-start | bytes 18440 | tf_op jit(solution)/shard_map/ppermute | solution.py:15
  55.5 148.9 %collective-permute-start.5 = (bf16[127,512]{1,0:T(8,128)(2,1)}, bf16[127,512]{1,0:T(8,128)(2,1)}, u32[]{:S(2)}, u32[]{:S(2)}) collective-permute-start(bf16[127,512]{1,0:T(8,128)(2,1)} %slice_bitcast_fusion.3), channel_id=1, source_target_pairs={{0,8},{8,16},{16,24},{24,32},{32,40},{40,48},{48,56},{56,64},{64,7... | collective-permute-start | bytes 390152 | tf_op jit(solution)/shard_map/ppermute | solution.py:15
  194.6 6.6 %copy-start.6 = (f32[136]{0:T(256)S(1)}, f32[136]{0:T(256)}, u32[]{:S(2)}) copy-start(f32[136]{0:T(256)} %copy-done.5) | copy-start | bytes 1636
  194.6 6.6 %copy-start.8 = (f32[136]{0:T(256)S(1)}, f32[136]{0:T(256)}, u32[]{:S(2)}) copy-start(f32[136]{0:T(256)} %copy-done.7) | copy-start | bytes 1636
  194.6 6.6 %copy-start.9 = (f32[136]{0:T(256)S(1)}, f32[136]{0:T(256)}, u32[]{:S(2)}) copy-start(f32[136]{0:T(256)} %get-tuple-element.40) | copy-start | bytes 1636
  194.6 6.6 %copy-start.10 = (f32[136]{0:T(256)S(1)}, f32[136]{0:T(256)}, u32[]{:S(2)}) copy-start(f32[136]{0:T(256)} %get-tuple-element.41) | copy-start | bytes 1636
  194.7 6.6 %copy-start.11 = (f32[136]{0:T(256)S(1)}, f32[136]{0:T(256)}, u32[]{:S(2)}) copy-start(f32[136]{0:T(256)} %get-tuple-element.42) | copy-start | bytes 1636
  194.7 6.6 %copy-start.12 = (f32[136]{0:T(256)S(1)}, f32[136]{0:T(256)}, u32[]{:S(2)}) copy-start(f32[136]{0:T(256)} %get-tuple-element.46) | copy-start | bytes 1636
  194.7 10.8 %copy-start.3 = (pred[136,263]{1,0:T(8,128)(4,1)S(1)}, pred[136,263]{1,0:T(8,128)(4,1)}, u32[]{:S(2)}) copy-start(pred[136,263]{1,0:T(8,128)(4,1)} %get-tuple-element.38) | copy-start | bytes 107308
  194.7 10.8 %copy-start.4 = (pred[136,263]{1,0:T(8,128)(4,1)S(1)}, pred[136,263]{1,0:T(8,128)(4,1)}, u32[]{:S(2)}) copy-start(pred[136,263]{1,0:T(8,128)(4,1)} %get-tuple-element.39) | copy-start | bytes 107308
  247.0 18.5 %copy-start.2 = (bf16[136,2,128]{2,1,0:T(2,128)(2,1)S(1)}, bf16[136,2,128]{2,1,0:T(2,128)(2,1)}, u32[]{:S(2)}) copy-start(bf16[136,2,128]{2,1,0:T(2,128)(2,1)} %reshape_squeeze.9) | copy-start | bytes 208900
  247.0 24.4 %slice-start = ((s8[4456448]{0:T(1024)(128)(4,1)}), s8[262144]{0:T(1024)(128)(4,1)S(1)}, s32[]{:S(2)}) async-start(s8[4456448]{0:T(1024)(128)(4,1)} %bitcast.121), calls=%async_computation.2 | async-start | bytes 524288
  265.5 5.9 %slice-start.1 = ((s8[4456448]{0:T(1024)(128)(4,1)}), s8[4194304]{0:T(1024)(128)(4,1)S(1)}, s32[]{:S(2)}) async-start(s8[4456448]{0:T(1024)(128)(4,1)} %bitcast.121), calls=%async_computation.3 | async-start | bytes 8388608
Sparse Core Ops, SparseCore 0:
  10.9 158.9 all-gather.1
where the time goes:
time: 283 us; the launch traced here: 281 us
  local copies, waits for them, and re-layouts  209 us (74%)
  starting transfers between devices  30.4 us (11%)
  other arithmetic  16.9 us (6%)
  between operations  14.5 us (5%)
  matrix products  9.42 us (3%)
    gather x3, local copies, waits for them, and re-layouts, banded_product(): toeplitz = jnp.take(filters, jnp.clip(lag_table, 0, span - 1), axis=0)  140 us
    unnamed x39, local copies, waits for them, and re-layouts  39.9 us
    ppermute x6, starting transfers between devices, from_behind(): return lax.ppermute(x, axis, pairs)  25.5 us
    slice x1, local copies, waits for them, and re-layouts, attend(): key_rows = portion[:, 0].reshape(count, head_count, HD)  18.7 us
  transfers between devices with their start and end apart: 8, of which 1 were waited for; matrix products, arithmetic and copies ran while one was open for 60% of the time, Pallas kernels for 0%

commit v1 on v0

v1 whole, which is shorter than its diff:
```python
import functools
import math

import jax
import jax.numpy as jnp
from jax import lax
from jax.experimental import pallas as pl
from jax.experimental.pallas import tpu as pltpu
from jax.sharding import PartitionSpec as P

NY, NZ, NCH = 4, 16, 8
ROWS = 136
HD = 128
QW = 640
COEF = math.log2(math.e) / math.sqrt(HD)
MESH = pl.DeviceIdType.MESH
BF, F32 = jnp.bfloat16, jnp.float32
TILES = ((0, 256), (256, 256), (512, 128))


def iota(shape, dim):
    return lax.broadcasted_iota(jnp.int32, shape, dim)


def kernel(
    qkv, x0, x1, x2, wf, sf, lf, posl, posc,
    attn, out0, out1, out2,
    qb, kv, pv, xv, rim, lfb, xf, mx, mx2, gate, ml, msend, rimm, mT, cT, cg, erev,
    qall, acc, mrow, lrow, tq, ds, of32, ob, orecv, auxs, auxr,
    loc, ksend, krecv, qsend, qrecv, psend, precv, rsend, rrecv, fsend, frecv,
    mssem, mrsem, osend, osrecv, asend, arecv,
):
    me = lax.axis_index("ctx")
    ch = lax.axis_index("ch")
    y, z = me // NZ, me % NZ
    xs = (x0, x1, x2)

    def zdev(k):
        return y * NZ + (z + k + NZ) % NZ

    def ydev(k):
        return ((y + k) % NY) * NZ + z

    nxt, prv = (me + 1) % (NY * NZ), (me + NY * NZ - 1) % (NY * NZ)

    def rcopy(src, dst, ss, rs, **dev):
        return pltpu.make_async_remote_copy(
            src_ref=src, dst_ref=dst, send_sem=ss, recv_sem=rs, device_id=dev, device_id_type=MESH
        )

    locals_ = [
        pltpu.make_async_copy(qkv.at[pl.ds(1, 2)], kv.at[z], loc.at[0]),
        pltpu.make_async_copy(qkv.at[0], qb.at[0], loc.at[1]),
        pltpu.make_async_copy(posl.at[0], pv.at[0], loc.at[2]),
        pltpu.make_async_copy(lf, lfb.at[ch], loc.at[3]),
    ] + [pltpu.make_async_copy(xs[i], xv.at[i], loc.at[4 + i]) for i in range(3)]
    for c in locals_:
        c.start()

    bar = pltpu.get_barrier_semaphore()
    peers = [zdev(1), zdev(-1), ydev(1), ydev(2), ydev(3), nxt, prv]
    for p in peers:
        pl.semaphore_signal(bar, inc=1, device_id={"ctx": p}, device_id_type=MESH)
    for d in range(1, NCH):
        pl.semaphore_signal(bar, inc=1, device_id={"ch": (ch + d) % NCH}, device_id_type=MESH)
    pl.semaphore_wait(bar, len(peers) + NCH - 1)

    def kvcopy(d, s, c):
        blk = (z - s + 1 + NZ) % NZ if d == 0 else (z + s - 1) % NZ
        tgt = zdev(1) if d == 0 else zdev(-1)
        return rcopy(kv.at[blk, c], kv.at[blk, c], ksend.at[d, s - 1, c], krecv.at[d, s - 1, c], ctx=tgt)

    def kvwait(d, s, c):
        blk = (z - s + NZ) % NZ if d == 0 else (z + s) % NZ
        rcopy(kv.at[blk, c], kv.at[blk, c], ksend.at[d, s - 1, c], krecv.at[d, s - 1, c], ctx=prv).wait_recv()

    locals_[0].wait()
    for c in range(2):
        for d in range(2):
            kvcopy(d, 1, c).start()
    raw = [rcopy(xs[i].at[:, pl.ds(128, 8), :], rim.at[i], rsend.at[i], rrecv.at[i], ctx=nxt) for i in range(3)]
    for i in (2, 0, 1):
        raw[i].start()
    locals_[1].wait()
    locals_[2].wait()
    locals_[3].wait()
    qs = [rcopy(qb.at[0], qb.at[r], qsend.at[r - 1], qrecv.at[r - 1], ctx=ydev(4 - r)) for r in range(1, 4)]
    ps = [rcopy(posl.at[r], pv.at[r], psend.at[r - 1], precv.at[r - 1], ctx=ydev(4 - r)) for r in range(1, 4)]
    fs = [
        rcopy(lfb.at[ch], lfb.at[ch], fsend.at[d - 1], frecv.at[d - 1], ch=(ch + d) % NCH)
        for d in range(1, NCH)
    ]
    for c in qs + ps + fs:
        c.start()
    for i in range(3):
        locals_[4 + i].wait()

    acc[...] = jnp.zeros_like(acc)
    mrow[...] = jnp.full_like(mrow, -1e20)
    lrow[...] = jnp.zeros_like(lrow)

    for c in qs + ps:
        c.wait_recv()
    lane = iota((8, QW), 1)
    b = (
        (lane >= ROWS).astype(jnp.int32)
        + (lane >= 2 * ROWS).astype(jnp.int32)
        + (lane >= 3 * ROWS).astype(jnp.int32)
    )
    yq = (y + b) % NY
    t_all = (yq * NZ + z) * ROWS + lane - ROWS * b
    tq[...] = t_all
    ds[...] = t_all - (pv[0] + pv[1] + pv[2] + pv[3])
    of32[pl.ds(544, 96), :] = jnp.zeros((96, 256), F32)
    for r in range(4):
        of32[pl.ds(ROWS * r, ROWS), :] = qb[r].astype(F32)
    qall[...] = of32[...].astype(BF)

    def att(blocks):
        for h in range(2):
            hs = pl.ds(h * HD, HD)
            ks = [kv[blk, 0, :, hs] for blk in blocks]
            vs = [kv[blk, 1, :, hs] for blk in blocks]
            for lo, w in TILES:
                cs = pl.ds(lo, w)
                q = qall[cs, hs]
                t_row, d_row = tq[0:1, cs], ds[0:1, cs]
                scores = []
                m_old = mrow[h : h + 1, cs]
                m_new = m_old
                for blk, k in zip(blocks, ks):
                    s = lax.dot_general(k, q, (((1,), (1,)), ((), ())), preferred_element_type=F32)
                    kid = (y * NZ + blk) * ROWS + iota((ROWS, w), 0)
                    s = jnp.where((kid <= t_row) & (kid >= d_row), s, -1e30)
                    scores.append(s)
                    m_new = jnp.maximum(m_new, jnp.max(s, axis=0, keepdims=True))
                alpha = jnp.exp2((m_old - m_new) * COEF)
                l_new = lrow[h : h + 1, cs] * alpha
                o_new = acc[h, :, cs] * alpha
                for s, v in zip(scores, vs):
                    p = jnp.exp2((s - m_new) * COEF)
                    l_new = l_new + jnp.sum(p, axis=0, keepdims=True)
                    o_new = o_new + lax.dot_general(
                        v, p.astype(BF), (((0,), (0,)), ((), ())), preferred_element_type=F32
                    )
                mrow[h : h + 1, cs] = m_new
                lrow[h : h + 1, cs] = l_new
                acc[h, :, cs] = o_new

    def features(i, lanes):
        out = []
        pos = posc[pl.ds(8, 144), :]
        for a in range(3):
            xf[a, pl.ds(0, 8), :] = jnp.zeros((8, 128), F32)
            xf[a, pl.ds(8, 8), :] = jnp.where(me > 0, rim[i, a, :, lanes].astype(F32), 0.0)
            xf[a, pl.ds(16, ROWS), :] = xv[i, a, :, lanes].astype(F32)
            tot = jnp.zeros((144, 128), F32)
            for j in range(3):
                row = (i * 3 + j) * 3 + a
                term = wf[row : row + 1, lanes] * xf[a, pl.ds(8 - j, 144), :]
                tot = tot + (jnp.where(pos >= j, term, 0.0) if j else term)
            out.append(tot)
        mixed = (out[1] * out[2]).astype(BF).astype(F32)
        return out[0][8:], mixed

    def lanes_of(lt):
        return pl.ds(pl.multiple_of(lt * 128, 128), 128)

    def short_layer(i, out):
        def unit(lt, carry):
            lanes = lanes_of(lt)
            g, mixed = features(i, lanes)
            mx[...] = mixed
            pos = posc[pl.ds(16, ROWS), :]
            tot = jnp.zeros((ROWS, 128), F32)
            for j in range(7):
                row = i * 7 + j
                term = sf[row : row + 1, lanes] * mx[pl.ds(8 - j, ROWS), :]
                tot = tot + (jnp.where(pos >= j, term, 0.0) if j else term)
            out[:, lanes] = (g * tot).astype(BF)
            return carry
        lax.fori_loop(0, 4, unit, 0)

    def long_features():
        def unit(lt, carry):
            lanes = lanes_of(lt)
            g, mixed = features(2, lanes)
            gate[:, lanes] = g
            ml[:, lanes] = mixed[8:]
            msend[:, lanes] = mixed[16:].astype(BF)
            return carry
        lax.fori_loop(0, 4, unit, 0)

    mcopy = rcopy(msend, rimm, mssem.at[0], mrsem.at[0], ctx=nxt)

    def long_filters():
        taps = lfb[...].reshape(128, 256)
        sel = (iota((32, 256), 1) == 32 * ch + iota((32, 256), 0)).astype(BF)
        cg[...] = lax.dot_general(sel, taps, (((1,), (1,)), ((), ())), preferred_element_type=F32)
        selc = (iota((256, 512), 0) == 32 * ch + (iota((256, 512), 1) >> 4)).astype(BF)
        wide = jnp.dot(taps, selc, preferred_element_type=F32).astype(BF)
        rev = (iota((128, 128), 0) + iota((128, 128), 1) == 127).astype(BF)
        erev[...] = jnp.dot(rev, wide, preferred_element_type=F32)

    def long_conv():
        prow = pv[0, 0:1, 0:128]
        pi, ti = iota((128, 128), 0), iota((128, 128), 1)
        top = ((ti < pi) & (ti + 128 - pi <= prow)).astype(F32)
        bot = ((ti >= pi) & (ti - pi <= prow)).astype(F32)

        def unit(lt, carry):
            lanes = lanes_of(lt)
            rm = jnp.where(me > 0, rimm[:, lanes].astype(F32), 0.0)
            loc_m = ml[:, lanes]
            mx2[pl.ds(0, 128), :] = rm
            mx2[pl.ds(128, ROWS), :] = loc_m
            mT[:, pl.ds(0, 128)] = rm.T.astype(BF)
            mT[:, pl.ds(128, 128)] = loc_m[:128].T.astype(BF)

            for g in range(8):
                f = jnp.broadcast_to(cg[pl.ds(lt * 8 + g, 1), :], (128, 128))
                r = pltpu.roll(f, 0, 1, stride=1, stride_axis=0)
                tt = jnp.concatenate([(r * top).astype(BF), (r * bot).astype(BF)], axis=0)
                cT[pl.ds(g * 16, 16), :] = jnp.dot(mT[pl.ds(g * 16, 16), :], tt, preferred_element_type=F32)
            conv = cT[...].T
            out2[pl.ds(0, 128), lanes] = (gate[pl.ds(0, 128), lanes] * conv).astype(BF)
            er = erev[:, lanes]
            back = 127 - iota((128, 128), 0)
            rows = []
            for i in range(8):
                pos = posc[pl.ds(144 + i, 1), :]
                term = jnp.where(back <= pos, er * mx2[pl.ds(129 + i, 128), :], 0.0)
                rows.append(jnp.sum(term, axis=0, keepdims=True))
            tail = jnp.concatenate(rows, axis=0)
            out2[pl.ds(128, 8), lanes] = (gate[pl.ds(128, 8), lanes] * tail).astype(BF)
            return carry
        lax.fori_loop(0, 4, unit, 0)

    def forward(s):
        for c in range(2):
            for d in range(2):
                kvwait(d, s, c)
                if d == 0:
                    @pl.when(s < 7)
                    def _():
                        kvcopy(0, s + 1, c).start()
                else:
                    kvcopy(1, s + 1, c).start()

    att([z])

    def step(s, carry):
        forward(s)
        att([(z - s + NZ) % NZ, (z + s) % NZ])

        @pl.when(s == 1)
        def _():
            for i in (2, 0, 1):
                raw[i].wait_recv()
            long_features()
            for c in fs:
                c.wait_recv()

        @pl.when(s == 2)
        def _():
            long_filters()
            mcopy.start()

        @pl.when(s == 3)
        def _():
            short_layer(0, out0)

        @pl.when(s == 4)
        def _():
            short_layer(1, out1)

        @pl.when(s == 5)
        def _():
            mcopy.wait_recv()
            long_conv()

        return carry

    lax.fori_loop(1, 8, step, 0)
    for c in range(2):
        kvwait(1, 8, c)
    att([(z + 8) % NZ])

    auxs[...] = jnp.zeros_like(auxs)
    auxs[0:2, :] = mrow[0:2, :]
    auxs[2:4, :] = lrow[0:2, :]
    aux_copies = [rcopy(auxs, auxr.at[4 - r], asend.at[r - 1], arecv.at[3 - r], ctx=ydev(r)) for r in range(1, 4)]
    for h in range(2):
        for k in range(5):
            of32[pl.ds(k * 128, 128), pl.ds(h * HD, HD)] = acc[h, :, pl.ds(k * 128, 128)].T
    for r in range(1, 4):
        ob[r - 1] = of32[pl.ds(ROWS * r, ROWS), :].astype(BF)
    o_copies = [rcopy(ob.at[r - 1], orecv.at[3 - r], osend.at[r - 1], osrecv.at[3 - r], ctx=ydev(r)) for r in range(1, 4)]
    for c in aux_copies + o_copies:
        c.start()
    for c in aux_copies:
        c.wait_recv()
    ms, ls = [auxs[0:2, 0:256]], [auxs[2:4, 0:256]]
    for k in range(1, 4):
        shifted = pltpu.roll(auxr[k], QW - ROWS * (4 - k), 1)[:, 0:256]
        ms.append(shifted[0:2])
        ls.append(shifted[2:4])
    top_m = functools.reduce(jnp.maximum, ms)
    es = [jnp.exp2((m - top_m) * COEF) for m in ms]
    den = functools.reduce(jnp.add, [e * l for e, l in zip(es, ls)])
    den = jnp.where(den > 0, den, 1.0)
    ws = jnp.concatenate([e / den for e in es] + [jnp.zeros((120, 256), F32)], axis=0)
    wt = jnp.concatenate([ws[:, :128].T, ws[:, 128:].T], axis=0)[:ROWS]
    for c in o_copies:
        c.wait_recv()
    for h in range(2):
        hs = pl.ds(h * HD, HD)
        tot = of32[pl.ds(0, ROWS), hs] * wt[:, h : h + 1]
        for k in range(1, 4):
            tot = tot + orecv[k - 1, :, hs].astype(F32) * wt[:, 2 * k + h : 2 * k + h + 1]
        attn[:, hs] = tot.astype(BF)

    for c in raw + qs + ps + fs + [mcopy] + aux_copies + o_copies:
        c.wait_send()
    for s in range(1, 9):
        for c in range(2):
            for d in range(2):
                if d == 1 or s < 8:
                    kvcopy(d, s, c).wait_send()


def body(attn_proj, first_in, second_in, third_in, feat_filters, short_filters, long_filter, positions):
    t3 = lambda v: jnp.transpose(v, (1, 0, 2))
    wf = jnp.pad(feat_filters.reshape(27, 512).astype(F32), ((0, 5), (0, 0)))
    sf = jnp.pad(jnp.repeat(short_filters.astype(F32).reshape(14, 32), 16, axis=1), ((0, 2), (0, 0)))
    posl = jnp.stack(
        [jnp.broadcast_to(jnp.pad(positions, (ROWS * r, QW - ROWS * (r + 1)))[None], (8, QW)) for r in range(4)]
    )
    ext = jnp.concatenate([positions[0] + jnp.arange(-16, 0, dtype=jnp.int32), positions])
    posc = jnp.broadcast_to(ext[:, None], (152, 128))
    vm = pl.BlockSpec(memory_space=pltpu.VMEM)
    hbm = pl.BlockSpec(memory_space=pl.ANY)
    dma = pltpu.SemaphoreType.DMA
    v = pltpu.VMEM
    return pl.pallas_call(
        kernel,
        out_shape=(
            jax.ShapeDtypeStruct((ROWS, 256), BF),
            jax.ShapeDtypeStruct((ROWS, 512), BF),
            jax.ShapeDtypeStruct((ROWS, 512), BF),
            jax.ShapeDtypeStruct((ROWS, 512), BF),
        ),
        in_specs=[hbm, hbm, hbm, hbm, vm, vm, hbm, hbm, vm],
        out_specs=[vm] * 4,
        scratch_shapes=[
            v((4, ROWS, 256), BF),
            v((NZ, 2, ROWS, 256), BF),
            v((4, 8, QW), jnp.int32),
            v((3, 3, ROWS, 512), BF),
            v((3, 3, 8, 512), BF),
            v((8, 16, 256), BF),
            v((3, 152, 128), F32),
            v((144, 128), F32),
            v((264, 128), F32),
            v((ROWS, 512), F32),
            v((ROWS, 512), F32),
            v((128, 512), BF),
            v((128, 512), BF),
            v((128, 256), BF),
            v((128, 128), F32),
            v((32, 128), F32),
            v((128, 512), F32),
            v((QW, 256), BF),
            v((2, HD, QW), F32),
            v((8, QW), F32),
            v((8, QW), F32),
            v((8, QW), jnp.int32),
            v((8, QW), jnp.int32),
            v((QW, 256), F32),
            v((3, ROWS, 256), BF),
            v((3, ROWS, 256), BF),
            v((8, QW), F32),
            v((4, 8, QW), F32),
            dma((7,)),
            dma((2, 8, 2)),
            dma((2, 8, 2)),
            dma((3,)),
            dma((3,)),
            dma((3,)),
            dma((3,)),
            dma((3,)),
            dma((3,)),
            dma((7,)),
            dma((7,)),
            dma((1,)),
            dma((1,)),
            dma((3,)),
            dma((3,)),
            dma((3,)),
            dma((3,)),
        ],
        compiler_params=pltpu.CompilerParams(collective_id=0, has_side_effects=True, vmem_limit_bytes=48 << 20),
        name="mixer",
    )(t3(attn_proj), t3(first_in), t3(second_in), t3(third_in), wf, sf, long_filter, posl, posc)


def solution(mesh):
    in_specs = (
        P("ctx", None, "ch"),
        P("ctx", None, "ch"),
        P("ctx", None, "ch"),
        P("ctx", None, "ch"),
        P(None, None, None, "ch"),
        P(None, None, "ch"),
        P("ch", None),
        P("ctx"),
    )
    out_specs = (P("ctx", "ch"), P("ctx", "ch"), P("ctx", "ch"), P("ctx", "ch"))
    return jax.shard_map(body, mesh=mesh, in_specs=in_specs, out_specs=out_specs, check_vma=False)
```

time: 283 us -> 67 us (0.24)
  the two profiles are of different devices: /device:TPU:82 before, /device:TPU:2 now
where the time goes in v1:
time: 67 us; the launch traced here: 66.8 us
  Pallas kernels  58.1 us (87%)
  local copies, waits for them, and re-layouts  7.21 us (11%)
  between operations  0.76 us (1%)
  other arithmetic  0.74 us (1%)
    pallas_call x1, Pallas kernels, body(): pl.pallas_call(kernel, out_shape=(jax.ShapeDtypeStruct((ROWS, 256), BF),...  58.1 us
    unnamed x20, local copies, waits for them, and re-layouts  5.55 us

profile of v1, /device:TPU:2, one launch (start us, length us, event | category | flops | bytes accessed | tf_op | source)
XLA Modules:
  0.0 66.8 jit_solution(390066041026866834)
XLA Ops:
  0.6 1.2 %slice.3 = s32[1]{0:T(128)} slice(s32[136]{0:T(256)} %param.15), slice={[0:1]} | slice | bytes 8 | tf_op jit(solution)/shard_map/slice | solution.py:339
  1.8 0.6 add_add_fusion
  2.5 0.0 copy-start.7
  2.5 0.0 copy-start.6
  2.5 0.7 %copy-done.6 = s32[136]{0:T(256)S(1)} copy-done((s32[136]{0:T(256)S(1)}, s32[136]{0:T(256)}, u32[]{:S(2)}) %copy-start.6) | copy-done | bytes 568
  3.2 0.1 pad_add_fusion.1
  3.3 0.0 copy-done.7
  3.3 0.0 copy-start.5
  3.3 0.1 fusion
  3.3 0.0 copy-start.4
  3.3 0.0 copy-start.3
  3.4 0.0 copy-start.1
  3.4 0.6 copy-done.5
  4.0 0.0 copy-start
  4.1 0.1 broadcast_in_dim.5.posc
  4.2 0.1 broadcast_in_dim.4
  4.3 0.1 reshape.23
  4.5 0.0 copy-done.4
  4.5 0.0 copy-done.3
  4.5 0.0 copy-done.1
  4.5 0.6 copy-done
  5.1 0.0 copy-start.2
  5.1 1.0 %copy-done.2 = bf16[136,3,512]{2,0,1:T(8,128)(2,1)S(1)} copy-done((bf16[136,3,512]{2,0,1:T(8,128)(2,1)S(1)}, bf16[136,3,512]{2,0,1:T(8,128)(2,1)}, u32[]{:S(2)}) %copy-start.2) | copy-done | bytes 417816
  6.1 58.1 %mixer.1 = (bf16[136,256]{1,0:T(8,128)(2,1)S(1)}, bf16[136,512]{1,0:T(8,128)(2,1)S(1)}, bf16[136,512]{1,0:T(8,128)(2,1)S(1)}, bf16[136,512]{1,0:T(8,128)(2,1)S(1)}) custom-call(bf16[3,136,256]{2,1,0:T(8,128)(2,1)S(1)} %bitcast.8, bf16[3,136,512]{2,1,0:T(8,128)(2,1)S(1)} %bitcast.5, bf16[3,136,512]{2,1,0:T(8,128)(2,1)S(1)} %bitcast.6, ...), custom_call_target="tpu_custom_call" | custom-call | tf_op jit(solution)/shard_map/mixer/pallas_call | solution.py:345
  64.2 0.6 copy.17
  64.8 0.7 copy.18
  65.5 0.7 copy.19
  66.1 0.7 copy.20
  (10 shorter events, 0.1 us)
Async XLA Ops:
  2.5 0.8 %copy-start.7 = (bf16[2,7,32]{2,0,1:T(2,128)(2,1)S(1)}, bf16[2,7,32]{2,0,1:T(2,128)(2,1)}, u32[]{:S(2)}) copy-start(bf16[2,7,32]{2,0,1:T(2,128)(2,1)} %param.13) | copy-start | bytes 2692
  2.5 0.7 %copy-start.6 = (s32[136]{0:T(256)S(1)}, s32[136]{0:T(256)}, u32[]{:S(2)}) copy-start(s32[136]{0:T(256)} %param.15) | copy-start | bytes 1636
  3.3 0.8 %copy-start.5 = (bf16[3,3,3,512]{3,2,1,0:T(4,128)(2,1)S(1)}, bf16[3,3,3,512]{3,2,1,0:T(4,128)(2,1)}, u32[]{:S(2)}) copy-start(bf16[3,3,3,512]{3,2,1,0:T(4,128)(2,1)} %param.12) | copy-start | bytes 82948
  3.3 1.1 %copy-start.4 = (bf16[16,256]{1,0:T(8,128)(2,1)S(1)}, bf16[16,256]{1,0:T(8,128)(2,1)}, u32[]{:S(2)}) copy-start(bf16[16,256]{1,0:T(8,128)(2,1)} %lf.1) | copy-start | bytes 24580
  3.3 1.1 %copy-start.3 = (bf16[136,3,256]{2,0,1:T(8,128)(2,1)S(1)}, bf16[136,3,256]{2,0,1:T(8,128)(2,1)}, u32[]{:S(2)}) copy-start(bf16[136,3,256]{2,0,1:T(8,128)(2,1)} %param.8) | copy-start | bytes 626692
  3.4 1.1 %copy-start.1 = (bf16[136,3,512]{2,0,1:T(8,128)(2,1)S(1)}, bf16[136,3,512]{2,0,1:T(8,128)(2,1)}, u32[]{:S(2)}) copy-start(bf16[136,3,512]{2,0,1:T(8,128)(2,1)} %param.10) | copy-start | bytes 1253380
  4.0 1.1 %copy-start = (bf16[136,3,512]{2,0,1:T(8,128)(2,1)S(1)}, bf16[136,3,512]{2,0,1:T(8,128)(2,1)}, u32[]{:S(2)}) copy-start(bf16[136,3,512]{2,0,1:T(8,128)(2,1)} %param.9) | copy-start | bytes 1253380
  5.1 1.0 %copy-start.2 = (bf16[136,3,512]{2,0,1:T(8,128)(2,1)S(1)}, bf16[136,3,512]{2,0,1:T(8,128)(2,1)}, u32[]{:S(2)}) copy-start(bf16[136,3,512]{2,0,1:T(8,128)(2,1)} %param.11) | copy-start | bytes 1253380

commit v2 on v1

--- a/solution.py
+++ b/solution.py
@@ -23,10 +23,10 @@
 
 
 def kernel(
-    qkv, x0, x1, x2, wf, sf, lf, posl, posc,
+    qkv, x0, x1, x2, wf, sfr, lf, posr,
     attn, out0, out1, out2,
     qb, kv, pv, xv, rim, lfb, xf, mx, mx2, gate, ml, msend, rimm, mT, cT, cg, erev,
-    qall, acc, mrow, lrow, tq, ds, of32, ob, orecv, auxs, auxr,
+    qall, acc, mrow, lrow, tq, ds, of32, ob, orecv, auxs, auxr, posl, posc, sf, sfs,
     loc, ksend, krecv, qsend, qrecv, psend, precv, rsend, rrecv, fsend, frecv,
     mssem, mrsem, osend, osrecv, asend, arecv,
 ):
@@ -49,11 +49,15 @@
         )
 
     locals_ = [
-        pltpu.make_async_copy(qkv.at[pl.ds(1, 2)], kv.at[z], loc.at[0]),
-        pltpu.make_async_copy(qkv.at[0], qb.at[0], loc.at[1]),
-        pltpu.make_async_copy(posl.at[0], pv.at[0], loc.at[2]),
-        pltpu.make_async_copy(lf, lfb.at[ch], loc.at[3]),
-    ] + [pltpu.make_async_copy(xs[i], xv.at[i], loc.at[4 + i]) for i in range(3)]
+        pltpu.make_async_copy(qkv.at[1 + c, :, pl.ds(h * HD, HD)], kv.at[z, c, h], loc.at[2 * c + h])
+        for c in range(2)
+        for h in range(2)
+    ]
+    locals_ += [
+        pltpu.make_async_copy(qkv.at[0], qb.at[0], loc.at[4]),
+        pltpu.make_async_copy(lf, lfb.at[ch], loc.at[5]),
+    ]
+    locals_ += [pltpu.make_async_copy(xs[i], xv.at[i], loc.at[6 + i]) for i in range(3)]
     for c in locals_:
         c.start()
 
@@ -63,29 +67,49 @@
         pl.semaphore_signal(bar, inc=1, device_id={"ctx": p}, device_id_type=MESH)
     for d in range(1, NCH):
         pl.semaphore_signal(bar, inc=1, device_id={"ch": (ch + d) % NCH}, device_id_type=MESH)
+
+    own = jnp.concatenate([posr[...].astype(F32), jnp.zeros((1, QW - ROWS), F32)], axis=1)
+    wide_pos = jnp.broadcast_to(own, (8, QW))
+    for r in range(4):
+        posl[r] = (pltpu.roll(wide_pos, ROWS * r, 1) if r else wide_pos)[0:1]
+    head = jnp.broadcast_to(own[:, 0:128], (128, 128)).T
+    posc[pl.ds(16, 128), :] = head
+    posc[pl.ds(144, 8), :] = jnp.broadcast_to(own[:, 128:256], (128, 128)).T[0:8]
+    posc[pl.ds(8, 8), :] = head[0:1] + (iota((8, 128), 0) - 8).astype(F32)
+    sfs[...] = jnp.zeros_like(sfs)
+    for j in range(7):
+        sfs[pl.ds(j, 1), :] = sfr[j, 0:1, :].astype(F32)
+        sfs[pl.ds(8 + j, 1), :] = sfr[j, 1:2, :].astype(F32)
+    spread = (iota((32, 512), 0) == (iota((32, 512), 1) >> 4)).astype(BF)
+    sf[...] = jnp.dot(sfs[...].astype(BF), spread, preferred_element_type=F32)
+    acc[...] = jnp.zeros_like(acc)
+    mrow[...] = jnp.full_like(mrow, -1e20)
+    lrow[...] = jnp.zeros_like(lrow)
     pl.semaphore_wait(bar, len(peers) + NCH - 1)
+
+    def part(blk, c):
+        return kv.at[blk, c // 2, c % 2]
 
     def kvcopy(d, s, c):
         blk = (z - s + 1 + NZ) % NZ if d == 0 else (z + s - 1) % NZ
         tgt = zdev(1) if d == 0 else zdev(-1)
-        return rcopy(kv.at[blk, c], kv.at[blk, c], ksend.at[d, s - 1, c], krecv.at[d, s - 1, c], ctx=tgt)
+        return rcopy(part(blk, c), part(blk, c), ksend.at[d, s - 1, c], krecv.at[d, s - 1, c], ctx=tgt)
 
     def kvwait(d, s, c):
         blk = (z - s + NZ) % NZ if d == 0 else (z + s) % NZ
-        rcopy(kv.at[blk, c], kv.at[blk, c], ksend.at[d, s - 1, c], krecv.at[d, s - 1, c], ctx=prv).wait_recv()
-
-    locals_[0].wait()
-    for c in range(2):
+        rcopy(part(blk, c), part(blk, c), ksend.at[d, s - 1, c], krecv.at[d, s - 1, c], ctx=prv).wait_recv()
+
+    for c in range(4):
+        locals_[c].wait()
         for d in range(2):
             kvcopy(d, 1, c).start()
     raw = [rcopy(xs[i].at[:, pl.ds(128, 8), :], rim.at[i], rsend.at[i], rrecv.at[i], ctx=nxt) for i in range(3)]
     for i in (2, 0, 1):
         raw[i].start()
-    locals_[1].wait()
-    locals_[2].wait()
-    locals_[3].wait()
+    locals_[4].wait()
+    locals_[5].wait()
     qs = [rcopy(qb.at[0], qb.at[r], qsend.at[r - 1], qrecv.at[r - 1], ctx=ydev(4 - r)) for r in range(1, 4)]
-    ps = [rcopy(posl.at[r], pv.at[r], psend.at[r - 1], precv.at[r - 1], ctx=ydev(4 - r)) for r in range(1, 4)]
+    ps = [rcopy(posl.at[r], pv.at[r - 1], psend.at[r - 1], precv.at[r - 1], ctx=ydev(4 - r)) for r in range(1, 4)]
     fs = [
         rcopy(lfb.at[ch], lfb.at[ch], fsend.at[d - 1], frecv.at[d - 1], ch=(ch + d) % NCH)
         for d in range(1, NCH)
@@ -93,11 +117,7 @@
     for c in qs + ps + fs:
         c.start()
     for i in range(3):
-        locals_[4 + i].wait()
-
-    acc[...] = jnp.zeros_like(acc)
-    mrow[...] = jnp.full_like(mrow, -1e20)
-    lrow[...] = jnp.zeros_like(lrow)
+        locals_[6 + i].wait()
 
     for c in qs + ps:
         c.wait_recv()
@@ -110,7 +130,8 @@
     yq = (y + b) % NY
     t_all = (yq * NZ + z) * ROWS + lane - ROWS * b
     tq[...] = t_all
-    ds[...] = t_all - (pv[0] + pv[1] + pv[2] + pv[3])
+    all_pos = posl[0] + pv[0] + pv[1] + pv[2]
+    ds[...] = t_all - jnp.broadcast_to(all_pos, (8, QW)).astype(jnp.int32)
     of32[pl.ds(544, 96), :] = jnp.zeros((96, 256), F32)
     for r in range(4):
         of32[pl.ds(ROWS * r, ROWS), :] = qb[r].astype(F32)
@@ -119,8 +140,8 @@
     def att(blocks):
         for h in range(2):
             hs = pl.ds(h * HD, HD)
-            ks = [kv[blk, 0, :, hs] for blk in blocks]
-            vs = [kv[blk, 1, :, hs] for blk in blocks]
+            ks = [kv[blk, 0, h] for blk in blocks]
+            vs = [kv[blk, 1, h] for blk in blocks]
             for lo, w in TILES:
                 cs = pl.ds(lo, w)
                 q = qall[cs, hs]
@@ -156,8 +177,7 @@
             xf[a, pl.ds(16, ROWS), :] = xv[i, a, :, lanes].astype(F32)
             tot = jnp.zeros((144, 128), F32)
             for j in range(3):
-                row = (i * 3 + j) * 3 + a
-                term = wf[row : row + 1, lanes] * xf[a, pl.ds(8 - j, 144), :]
+                term = wf[i, j, a : a + 1, lanes].astype(F32) * xf[a, pl.ds(8 - j, 144), :]
                 tot = tot + (jnp.where(pos >= j, term, 0.0) if j else term)
             out.append(tot)
         mixed = (out[1] * out[2]).astype(BF).astype(F32)
@@ -174,7 +194,7 @@
             pos = posc[pl.ds(16, ROWS), :]
             tot = jnp.zeros((ROWS, 128), F32)
             for j in range(7):
-                row = i * 7 + j
+                row = i * 8 + j
                 term = sf[row : row + 1, lanes] * mx[pl.ds(8 - j, ROWS), :]
                 tot = tot + (jnp.where(pos >= j, term, 0.0) if j else term)
             out[:, lanes] = (g * tot).astype(BF)
@@ -203,10 +223,10 @@
         erev[...] = jnp.dot(rev, wide, preferred_element_type=F32)
 
     def long_conv():
-        prow = pv[0, 0:1, 0:128]
+        prow = posl[0, 0:1, 0:128]
         pi, ti = iota((128, 128), 0), iota((128, 128), 1)
-        top = ((ti < pi) & (ti + 128 - pi <= prow)).astype(F32)
-        bot = ((ti >= pi) & (ti - pi <= prow)).astype(F32)
+        top = ((ti < pi) & ((ti + 128 - pi).astype(F32) <= prow)).astype(F32)
+        bot = ((ti >= pi) & ((ti - pi).astype(F32) <= prow)).astype(F32)
 
         def unit(lt, carry):
             lanes = lanes_of(lt)
@@ -225,7 +245,7 @@
             conv = cT[...].T
             out2[pl.ds(0, 128), lanes] = (gate[pl.ds(0, 128), lanes] * conv).astype(BF)
             er = erev[:, lanes]
-            back = 127 - iota((128, 128), 0)
+            back = (127 - iota((128, 128), 0)).astype(F32)
             rows = []
             for i in range(8):
                 pos = posc[pl.ds(144 + i, 1), :]
@@ -237,7 +257,7 @@
         lax.fori_loop(0, 4, unit, 0)
 
     def forward(s):
-        for c in range(2):
+        for c in range(4):
             for d in range(2):
                 kvwait(d, s, c)
                 if d == 0:
@@ -282,14 +302,16 @@
         return carry
 
     lax.fori_loop(1, 8, step, 0)
-    for c in range(2):
+    for c in range(4):
         kvwait(1, 8, c)
     att([(z + 8) % NZ])
 
-    auxs[...] = jnp.zeros_like(auxs)
-    auxs[0:2, :] = mrow[0:2, :]
-    auxs[2:4, :] = lrow[0:2, :]
-    aux_copies = [rcopy(auxs, auxr.at[4 - r], asend.at[r - 1], arecv.at[3 - r], ctx=ydev(r)) for r in range(1, 4)]
+    both = jnp.concatenate([mrow[0:2, :], lrow[0:2, :], jnp.zeros((4, QW), F32)], axis=0)
+    for r in range(1, 4):
+        auxs[r - 1] = pltpu.roll(both, QW - ROWS * r, 1)[:, 0:256]
+    aux_copies = [
+        rcopy(auxs.at[r - 1], auxr.at[3 - r], asend.at[r - 1], arecv.at[3 - r], ctx=ydev(r)) for r in range(1, 4)
+    ]
     for h in range(2):
         for k in range(5):
             of32[pl.ds(k * 128, 128), pl.ds(h * HD, HD)] = acc[h, :, pl.ds(k * 128, 128)].T
@@ -300,11 +322,10 @@
         c.start()
     for c in aux_copies:
         c.wait_recv()
-    ms, ls = [auxs[0:2, 0:256]], [auxs[2:4, 0:256]]
+    ms, ls = [both[0:2, 0:256]], [both[2:4, 0:256]]
     for k in range(1, 4):
-        shifted = pltpu.roll(auxr[k], QW - ROWS * (4 - k), 1)[:, 0:256]
-        ms.append(shifted[0:2])
-        ls.append(shifted[2:4])
+        ms.append(auxr[k - 1, 0:2, :])
+        ls.append(auxr[k - 1, 2:4, :])
     top_m = functools.reduce(jnp.maximum, ms)
     es = [jnp.exp2((m - top_m) * COEF) for m in ms]
     den = functools.reduce(jnp.add, [e * l for e, l in zip(es, ls)])
@@ -323,39 +344,47 @@
     for c in raw + qs + ps + fs + [mcopy] + aux_copies + o_copies:
         c.wait_send()
     for s in range(1, 9):
-        for c in range(2):
+        for c in range(4):
             for d in range(2):
                 if d == 1 or s < 8:
                     kvcopy(d, s, c).wait_send()
 
 
+def finish(outs):
+    def place(*refs):
+        sems = refs[8]
+        copies = [pltpu.make_async_copy(refs[i], refs[4 + i], sems.at[i]) for i in range(4)]
+        for c in copies:
+            c.start()
+        for c in copies:
+            c.wait()
+
+    return pl.pallas_call(
+        place,
+        out_shape=tuple(jax.ShapeDtypeStruct(o.shape, o.dtype) for o in outs),
+        in_specs=[pl.BlockSpec(memory_space=pltpu.VMEM)] * 4,
+        out_specs=[pl.BlockSpec(memory_space=pltpu.HBM)] * 4,
+        scratch_shapes=[pltpu.SemaphoreType.DMA((4,))],
+        compiler_params=pltpu.CompilerParams(vmem_limit_bytes=1 << 20),
+        name="finish",
+    )(*outs)
+
+
 def body(attn_proj, first_in, second_in, third_in, feat_filters, short_filters, long_filter, positions):
     t3 = lambda v: jnp.transpose(v, (1, 0, 2))
-    wf = jnp.pad(feat_filters.reshape(27, 512).astype(F32), ((0, 5), (0, 0)))
-    sf = jnp.pad(jnp.repeat(short_filters.astype(F32).reshape(14, 32), 16, axis=1), ((0, 2), (0, 0)))
-    posl = jnp.stack(
-        [jnp.broadcast_to(jnp.pad(positions, (ROWS * r, QW - ROWS * (r + 1)))[None], (8, QW)) for r in range(4)]
-    )
-    ext = jnp.concatenate([positions[0] + jnp.arange(-16, 0, dtype=jnp.int32), positions])
-    posc = jnp.broadcast_to(ext[:, None], (152, 128))
     vm = pl.BlockSpec(memory_space=pltpu.VMEM)
-    hbm = pl.BlockSpec(memory_space=pl.ANY)
+    hbm = pl.BlockSpec(memory_space=pltpu.HBM)
     dma = pltpu.SemaphoreType.DMA
     v = pltpu.VMEM
-    return pl.pallas_call(
+    outs = pl.pallas_call(
         kernel,
-        out_shape=(
-            jax.ShapeDtypeStruct((ROWS, 256), BF),
-            jax.ShapeDtypeStruct((ROWS, 512), BF),
-            jax.ShapeDtypeStruct((ROWS, 512), BF),
-            jax.ShapeDtypeStruct((ROWS, 512), BF),
-        ),
-        in_specs=[hbm, hbm, hbm, hbm, vm, vm, hbm, hbm, vm],
+        out_shape=(v((ROWS, 256), BF), v((ROWS, 512), BF), v((ROWS, 512), BF), v((ROWS, 512), BF)),
+        in_specs=[hbm, hbm, hbm, hbm, vm, vm, hbm, vm],
         out_specs=[vm] * 4,
         scratch_shapes=[
             v((4, ROWS, 256), BF),
-            v((NZ, 2, ROWS, 256), BF),
-            v((4, 8, QW), jnp.int32),
+            v((NZ, 2, 2, ROWS, HD), BF),
+            v((3, 1, QW), F32),
             v((3, 3, ROWS, 512), BF),
             v((3, 3, 8, 512), BF),
             v((8, 16, 256), BF),
@@ -379,11 +408,15 @@
             v((QW, 256), F32),
             v((3, ROWS, 256), BF),
             v((3, ROWS, 256), BF),
-            v((8, QW), F32),
-            v((4, 8, QW), F32),
-            dma((7,)),
-            dma((2, 8, 2)),
-            dma((2, 8, 2)),
+            v((3, 8, 256), F32),
+            v((3, 8, 256), F32),
+            v((4, 1, QW), F32),
+            v((152, 128), F32),
+            v((16, 512), F32),
+            v((16, 32), F32),
+            dma((9,)),
+            dma((2, 8, 4)),
+            dma((2, 8, 4)),
             dma((3,)),
             dma((3,)),
             dma((3,)),
@@ -399,9 +432,10 @@
             dma((3,)),
             dma((3,)),
         ],
-        compiler_params=pltpu.CompilerParams(collective_id=0, has_side_effects=True, vmem_limit_bytes=48 << 20),
+        compiler_params=pltpu.CompilerParams(collective_id=0, has_side_effects=True, vmem_limit_bytes=60_000_000),
         name="mixer",
-    )(t3(attn_proj), t3(first_in), t3(second_in), t3(third_in), wf, sf, long_filter, posl, posc)
+    )(t3(attn_proj), t3(first_in), t3(second_in), t3(third_in), feat_filters, t3(short_filters), long_filter, positions.reshape(1, ROWS))
+    return finish(outs)
 
 
 def solution(mesh):

time: 67 us -> 58.4 us (0.87)
  local copies, waits for them, and re-layouts: 7.21 us -> 0 us
  other arithmetic: 0.74 us -> 0 us
    unnamed x20 -> x0, local copies, waits for them, and re-layouts: 5.55 us -> none
    slice x1 -> x0, local copies, waits for them, and re-layouts: 1.19 us -> none  [body(): positions[0] + jnp.arange(-16, 0, dtype=jnp.int32)]
    pallas_call x1 -> x2, Pallas kernels: 58.1 us -> 57.5 us  [the longest x1 56.7 us: body(): pl.pallas_call(kernel, out_shape=(v((ROWS, 256), BF), v((ROWS, 512), BF),...]
where the time goes in v2:
time: 58.4 us; the launch traced here: 58.2 us
  Pallas kernels  57.5 us (98%)
  between operations  0.64 us (1%)
    pallas_call x1, Pallas kernels, body(): pl.pallas_call(kernel, out_shape=(v((ROWS, 256), BF), v((ROWS, 512), BF),...  56.7 us

profile of v2, /device:TPU:2, one launch (start us, length us, event | category | flops | bytes accessed | tf_op | source)
XLA Modules:
  0.0 58.2 jit_solution(10801164657954163323)
XLA Ops:
  0.6 56.7 %mixer.1 = (bf16[136,256]{1,0:T(8,128)(2,1)S(1)}, bf16[136,512]{1,0:T(8,128)(2,1)S(1)}, bf16[136,512]{1,0:T(8,128)(2,1)S(1)}, bf16[136,512]{1,0:T(8,128)(2,1)S(1)}) custom-call(bf16[3,136,256]{2,1,0:T(8,128)(2,1)} %bitcast.9, bf16[3,136,512]{2,1,0:T(8,128)(2,1)} %bitcast.6, bf16[3,136,512]{2,1,0:T(8,128)(2,1)} %bitcast.7, bf16[3,136,512]{2,1,0:T(8,128)(2,1)} %bitcast.8, ...), custom_call_target="tpu_custom_call" | custom-call | tf_op jit(solution)/shard_map/mixer/pallas_call | solution.py:379
  57.4 0.8 %finish.1 = (bf16[136,256]{1,0:T(8,128)(2,1)}, bf16[136,512]{1,0:T(8,128)(2,1)}, bf16[136,512]{1,0:T(8,128)(2,1)}, bf16[136,512]{1,0:T(8,128)(2,1)}) custom-call(bf16[136,256]{1,0:T(8,128)(2,1)S(1)} %get-tuple-element.8.refs_0_, bf16[136,512]{1,0:T(8,128)(2,1)S(1)} %get-tuple-element.9.refs_1_, bf16[136,512]{1,0:T(8,128)(2,1)S(1)} %get-tuple-element.10.refs_2_, ...), custom_call_target="tpu_custom_call" | custom-call | tf_op jit(solution)/shard_map/finish/pallas_call | solution.py:362
